TPU v7x, 256 devices: a whole 4x4x8 slice. The times are simulated.
256 devices in a mesh: dp: 4 (over y), pipe: 4 (over z_hi), tensor: 16 (over x, z_lo, core).
Axes of the slice: x: 4, y: 4, z: 8 (z_hi: 4, z_lo: 2; z = z_hi * 2 + z_lo), core: 2. Of those that a mesh axis runs over, the one named last changes fastest.
Arguments:
- hidden: bfloat16 [4, 2048, 14336], P('pipe', 'dp', 'tensor'), parts along dimension 1, may hold values from -6 to 6
- residual: bfloat16 [4, 2048, 4096], P('pipe', ('dp', 'tensor')), parts along dimension 1, may hold values from -6 to 6
- norm_gain: float32 [4, 4096], P('pipe'), may hold values from 0.5 to 1.5
- down_weight: bfloat16 [4, 14336, 4096], P('pipe', 'tensor'), may hold values from -0.046875 to 0.046875
- qkv_weight: bfloat16 [4, 4096, 6144], P('pipe', None, 'tensor'), may hold values from -0.09375 to 0.09375
Outputs:
- section_output: bfloat16 [4, 2048, 4096], P('pipe', ('dp', 'tensor')), parts along dimension 1
- projections: bfloat16 [4, 2048, 6144], P('pipe', 'dp', 'tensor'), parts along dimension 1
There are 4 independent parts, one for each index of `dp`. A program takes and returns all parts, laid end to end along the dimension named above; an argument that names none is the same for every part. Nothing has to cross between parts.
All inputs are finite; a program needn't handle non-finite values.
Results may differ from a plain program's by a relative error of at most 0.022.
Values may be sent and summed in bfloat16 or wider, within the bound.
No kernel may reach another device: no remote copies, remote signals or barrier semaphores. Data moves between devices by JAX's collectives and lax.ppermute only.
A program may use at most 64 MiB of HBM per device.

v0:
```python
import jax
import jax.numpy as jnp
from jax import lax
from jax.sharding import PartitionSpec as P


def passed_along(value, axis, steps):
    count = lax.axis_size(axis)
    pairs = [(source, (source + steps) % count) for source in range(count)]
    return lax.ppermute(value, axis, pairs)


def normalize(values, gain_row):
    wide = values.astype(jnp.float32)
    scaler = lax.rsqrt(jnp.mean(wide * wide, axis=-1, keepdims=True) + 1e-05)
    return (wide * scaler * gain_row).astype(jnp.bfloat16)


def shards(hidden, residual, norm_gain, down_weight, qkv_weight):
    hidden_rows = hidden[0]
    resid_rows = residual[0]
    gain_row = norm_gain[0]
    down_local = down_weight[0]
    qkv_local = qkv_weight[0]
    tok_rows = resid_rows.shape[0]
    resid_full = lax.all_gather(resid_rows, "tensor", axis=0, tiled=True)
    summed = lax.psum(
        jnp.dot(hidden_rows, down_local, preferred_element_type=jnp.float32).astype(jnp.bfloat16),
        "tensor",
    ).astype(jnp.float32)
    full_rows = (resid_full.astype(jnp.float32) + summed).astype(jnp.bfloat16)
    offset = lax.axis_index("tensor") * tok_rows
    section_output = lax.dynamic_slice_in_dim(full_rows, offset, tok_rows, 0)
    arrived = passed_along(full_rows, "pipe", 1)
    normed = normalize(arrived, gain_row)
    projections = jnp.dot(normed, qkv_local, preferred_element_type=jnp.float32).astype(
        jnp.bfloat16
    )
    return (section_output[None], projections[None])


def solution(mesh):
    return jax.shard_map(
        shards,
        mesh=mesh,
        in_specs=(
            P("pipe", "dp", "tensor"),
            P("pipe", ("dp", "tensor"), None),
            P("pipe", None),
            P("pipe", "tensor", None),
            P("pipe", None, "tensor"),
        ),
        out_specs=(P("pipe", ("dp", "tensor"), None), P("pipe", "dp", "tensor")),
        check_vma=False,
    )
```

profile of v0, /device:TPU:2, one launch (start us, length us, event | category | flops | bytes accessed | tf_op | source)
XLA Modules:
  0.0 410.3 jit_solution(18110407928350033155)
XLA Ops:
  7.2 0.0 copy-start
  7.2 0.0 all-reduce.2.cloned.1.call-start
  7.2 10.0 %fusion.6 = bf16[512,4096]{1,0:T(8,128)(2,1)} fusion(bf16[1,896,4096]{2,1,0:T(8,128)(2,1)} %param.8, bf16[1,512,896]{2,1,0:T(8,128)(2,1)} %param.5), kind=kOutput, calls=%fused_computation.9 | convolution fusion | flops 3760193536 | bytes 12451840 | tf_op jit(solution)/shard_map/dot_general | solution.py:28
  17.2 0.0 all-reduce.2.cloned.1.call-update
  17.2 0.0 all-gather.3.cloned.1.call-start
  17.3 0.7 all-gather.3.cloned.1.call-update
  18.0 137.3 %all-reduce.2.cloned.1.call-done = bf16[512,4096]{1,0:T(8,128)(2,1)} async-done(((bf16[512,4096]{1,0:T(8,128)(2,1)}), bf16[512,4096]{1,0:T(8,128)(2,1)}) %all-reduce.2.cloned.1.call-update) | async-done | bytes 4194320 | tf_op jit(solution)/shard_map/psum | solution.py:27
  155.2 46.2 %all-gather.3.cloned.1.call-done = bf16[1,512,4096]{2,1,0:T(8,128)(2,1)} async-done(((bf16[1,32,4096]{2,1,0:T(8,128)(2,1)}), bf16[1,512,4096]{2,1,0:T(8,128)(2,1)}) %all-gather.3.cloned.1.call-update) | async-done | bytes 4194320 | tf_op jit(solution)/shard_map/all_gather | solution.py:26
  201.5 7.2 %fusion.3 = bf16[512,4096]{1,0:T(8,128)(2,1)} fusion(bf16[512,4096]{1,0:T(8,128)(2,1)} %all-reduce.2.cloned.1.call-done, bf16[1,512,4096]{2,1,0:T(8,128)(2,1)} %all-gather.3.cloned.1.call-done), kind=kLoop, calls=%fused_computation.6 | loop fusion | flops 8388608 | bytes 12582912 | tf_op jit(solution)/shard_map/convert_element_type | solution.py:31
  208.6 0.0 copy-start.1
  208.6 2.6 collective-permute-start
  211.2 1.7 dynamic-slice_bitcast_fusion
  212.9 182.2 %collective-permute-done = bf16[512,4096]{1,0:T(8,128)(2,1)} collective-permute-done((bf16[512,4096]{1,0:T(8,128)(2,1)}, bf16[512,4096]{1,0:T(8,128)(2,1)}, u32[]{:S(2)}, u32[]{:S(2)}) %collective-permute-start) | collective-permute-done | bytes 4194336 | tf_op jit(solution)/shard_map/ppermute | solution.py:10
  395.1 3.1 fusion
  398.1 0.0 copy-done
  398.2 0.0 copy-done.1
  398.2 5.3 %fusion.19 = bf16[1,512,384]{2,1,0:T(8,128)(2,1)} fusion(bf16[1,4096,384]{2,1,0:T(8,128)(2,1)S(1)} %copy-done, bf16[512,4096]{1,0:T(8,128)(2,1)} %collective-permute-done, f32[4096]{0:T(1024)S(1)} %bitcast.23, f32[512]{0:T(512)S(1)} %add_rsqrt_fusion), kind=kOutput, calls=%fused_computation.15 | convolution fusion | flops 1619197952 | bytes 7751680 | tf_op jit(solution)/shard_map/dot_general | solution.py:36
  (1 shorter events, 0.0 us)
Async XLA Ops:
  7.2 391.0 %copy-start = (bf16[1,4096,384]{2,1,0:T(8,128)(2,1)S(1)}, bf16[1,4096,384]{2,1,0:T(8,128)(2,1)}, u32[]{:S(2)}) copy-start(bf16[1,4096,384]{2,1,0:T(8,128)(2,1)} %param.9) | copy-start | bytes 9437188
  7.2 148.1 %all-reduce.2.cloned.1.call-start = ((), (), s32[]{:S(2)}) async-start(), calls=%async_computation | async-start | bytes 8388608 | tf_op jit(solution)/shard_map/psum | solution.py:27
  17.2 184.2 %all-gather.3.cloned.1.call-start = ((), (), s32[]{:S(2)}) async-start(), calls=%async_computation.1 | async-start | bytes 4456448 | tf_op jit(solution)/shard_map/all_gather | solution.py:26
  208.6 189.5 %copy-start.1 = (f32[1,4096]{1,0:T(1,128)S(1)}, f32[1,4096]{1,0:T(1,128)}, u32[]{:S(2)}) copy-start(f32[1,4096]{1,0:T(1,128)} %param.7) | copy-start | bytes 49156
  208.6 186.4 %collective-permute-start = (bf16[512,4096]{1,0:T(8,128)(2,1)}, bf16[512,4096]{1,0:T(8,128)(2,1)}, u32[]{:S(2)}, u32[]{:S(2)}) collective-permute-start(bf16[512,4096]{1,0:T(8,128)(2,1)} %fusion.3), channel_id=1, source_target_pairs={{0,16},{16,32},{32,48},{48,0},{1,17},{17,33},{33,49},{49,1},{2,18}... | collective-permute-start | bytes 12582920 | tf_op jit(solution)/shard_map/ppermute | solution.py:10
Sparse Core Ops, SparseCore 0:
  17.3 137.8 all-reduce.1
  157.1 44.3 all-gather.2
where the time goes:
time: 410 us
  waiting for transfers between devices  366 us (89%)
  matrix products  15.3 us (4%)
  between operations  14.1 us (3%)
  other arithmetic  10.3 us (3%)
    ppermute x1, waiting for transfers between devices, passed_along(): return lax.ppermute(value, axis, pairs)  182 us
    psum x1, waiting for transfers between devices, shards(): lax.psum(jnp.dot(hidden_rows, down_local, preferred_element_type=jnp.floa...  137 us
    all_gather x1, waiting for transfers between devices, shards(): resid_full = lax.all_gather(resid_rows, 'tensor', axis=0, tiled=True)  46.2 us
    dot_general x1, matrix products, shards(): jnp.dot(hidden_rows, down_local, preferred_element_type=jnp.float32)  9.96 us
  transfers between devices with their start and end apart: 3, of which 3 were waited for; matrix products, arithmetic and copies ran while one was open for 0% of the time, Pallas kernels for 0%

commit v1 on v0

--- a/solution.py
+++ b/solution.py
@@ -23,7 +23,9 @@
     down_local = down_weight[0]
     qkv_local = qkv_weight[0]
     tok_rows = resid_rows.shape[0]
-    resid_full = lax.all_gather(resid_rows, "tensor", axis=0, tiled=True)
+    resid_full = jnp.concatenate(
+        lax.all_to_all(jnp.stack([resid_rows] * lax.axis_size("tensor")), "tensor", 0, 0), axis=0
+    )
     summed = lax.psum(
         jnp.dot(hidden_rows, down_local, preferred_element_type=jnp.float32).astype(jnp.bfloat16),
         "tensor",

time: 410 us -> 390 us (0.951)
  waiting for transfers between devices: 366 us -> 333 us
  starting transfers between devices: 2.64 us -> 9.13 us
    all_gather x1 -> x0, waiting for transfers between devices: 46.2 us -> none  [shards(): resid_full = lax.all_gather(resid_rows, 'tensor', axis=0, tiled=True)]
    psum x1, waiting for transfers between devices: 137 us -> 153 us  [shards(): lax.psum(jnp.dot(hidden_rows, down_local, preferred_element_type=jnp.floa...]
    all_to_all x0 -> x1, starting transfers between devices: none -> 6.55 us  [shards(): lax.all_to_all(jnp.stack([resid_rows] * lax.axis_size('tensor')), 'tensor...]
  transfers between devices with their start and end apart: 3 -> 3, of which waited for: 3 -> 2; matrix products, arithmetic and copies ran while one was open for 0% -> 3% of each run, Pallas kernels for 0% -> 0%
where the time goes in v1:
time: 390 us; the launch traced here: 387 us
  waiting for transfers between devices  333 us (85%)
  matrix products  15.1 us (4%)
  between operations  14.1 us (4%)
  other arithmetic  10.3 us (3%)
  starting transfers between devices  9.13 us (2%)
  local copies, waits for them, and re-layouts  5.28 us (1%)
    ppermute x1, waiting for transfers between devices, passed_along(): return lax.ppermute(value, axis, pairs)  180 us
    psum x1, waiting for transfers between devices, shards(): lax.psum(jnp.dot(hidden_rows, down_local, preferred_element_type=jnp.floa...  153 us
    dot_general x1, matrix products, shards(): jnp.dot(hidden_rows, down_local, preferred_element_type=jnp.float32)  9.83 us
  transfers between devices with their start and end apart: 3, of which 2 were waited for; matrix products, arithmetic and copies ran while one was open for 3% of the time, Pallas kernels for 0%

profile of v1, /device:TPU:2, one launch (start us, length us, event | category | flops | bytes accessed | tf_op | source)
XLA Modules:
  0.0 386.6 jit_solution(16743926435729313868)
XLA Ops:
  7.2 0.0 copy-start
  7.2 3.6 stack.3
  10.7 6.5 %all-to-all-start = ((bf16[16,32,4096]{2,1,0:T(8,128)(2,1)}), bf16[16,32,4096]{2,1,0:T(8,128)(2,1)}, u32[]{:S(2)}, u32[]{:S(2)}) async-start(bf16[16,32,4096]{2,1,0:T(8,128)(2,1)} %stack.3), calls=%async_computation | async-start | bytes 8388608 | tf_op jit(solution)/shard_map/all_to_all | solution.py:27
  17.3 0.0 all-reduce.2.cloned.1.call-start
  17.3 9.8 %fusion.6 = bf16[512,4096]{1,0:T(8,128)(2,1)} fusion(bf16[1,896,4096]{2,1,0:T(8,128)(2,1)} %param.8, bf16[1,512,896]{2,1,0:T(8,128)(2,1)} %param.5), kind=kOutput, calls=%fused_computation.9 | convolution fusion | flops 3760193536 | bytes 12451840 | tf_op jit(solution)/shard_map/dot_general | solution.py:30
  27.2 0.0 all-reduce.2.cloned.1.call-update
  27.2 153.1 %all-reduce.2.cloned.1.call-done = bf16[512,4096]{1,0:T(8,128)(2,1)} async-done(((bf16[512,4096]{1,0:T(8,128)(2,1)}), bf16[512,4096]{1,0:T(8,128)(2,1)}) %all-reduce.2.cloned.1.call-update) | async-done | bytes 4194320 | tf_op jit(solution)/shard_map/psum | solution.py:29
  180.3 0.0 all-to-all-done
  180.3 7.2 %fusion.3 = bf16[512,4096]{1,0:T(8,128)(2,1)} fusion(bf16[512,4096]{1,0:T(8,128)(2,1)} %all-reduce.2.cloned.1.call-done, bf16[16,32,4096]{2,1,0:T(8,128)(2,1)} %all-to-all-done), kind=kLoop, calls=%fused_computation.6 | loop fusion | flops 8388608 | bytes 12582912 | tf_op jit(solution)/shard_map/convert_element_type | solution.py:33
  187.5 0.0 copy-start.1
  187.5 2.5 collective-permute-start
  190.0 1.7 dynamic-slice_bitcast_fusion
  191.7 179.6 %collective-permute-done = bf16[512,4096]{1,0:T(8,128)(2,1)} collective-permute-done((bf16[512,4096]{1,0:T(8,128)(2,1)}, bf16[512,4096]{1,0:T(8,128)(2,1)}, u32[]{:S(2)}, u32[]{:S(2)}) %collective-permute-start) | collective-permute-done | bytes 4194336 | tf_op jit(solution)/shard_map/ppermute | solution.py:10
  371.3 3.1 fusion
  374.4 0.0 copy-done
  374.4 0.0 copy-done.1
  374.5 5.3 %fusion.19 = bf16[1,512,384]{2,1,0:T(8,128)(2,1)} fusion(bf16[1,4096,384]{2,1,0:T(8,128)(2,1)S(1)} %copy-done, bf16[512,4096]{1,0:T(8,128)(2,1)} %collective-permute-done, f32[4096]{0:T(1024)S(1)} %bitcast.25, f32[512]{0:T(512)S(1)} %add_rsqrt_fusion), kind=kOutput, calls=%fused_computation.15 | convolution fusion | flops 1619197952 | bytes 7751680 | tf_op jit(solution)/shard_map/dot_general | solution.py:38
  (1 shorter events, 0.0 us)
Async XLA Ops:
  7.2 367.3 %copy-start = (bf16[1,4096,384]{2,1,0:T(8,128)(2,1)S(1)}, bf16[1,4096,384]{2,1,0:T(8,128)(2,1)}, u32[]{:S(2)}) copy-start(bf16[1,4096,384]{2,1,0:T(8,128)(2,1)} %param.9) | copy-start | bytes 9437188
  10.7 169.5 %all-to-all-start = ((bf16[16,32,4096]{2,1,0:T(8,128)(2,1)}), bf16[16,32,4096]{2,1,0:T(8,128)(2,1)}, u32[]{:S(2)}, u32[]{:S(2)}) async-start(bf16[16,32,4096]{2,1,0:T(8,128)(2,1)} %stack.3), calls=%async_computation | async-start | bytes 8388608 | tf_op jit(solution)/shard_map/all_to_all | solution.py:27
  17.3 163.0 %all-reduce.2.cloned.1.call-start = ((), (), s32[]{:S(2)}) async-start(), calls=%async_computation.1 | async-start | bytes 8388608 | tf_op jit(solution)/shard_map/psum | solution.py:29
  187.5 187.0 %copy-start.1 = (f32[1,4096]{1,0:T(1,128)S(1)}, f32[1,4096]{1,0:T(1,128)}, u32[]{:S(2)}) copy-start(f32[1,4096]{1,0:T(1,128)} %param.7) | copy-start | bytes 49156
  187.5 183.9 %collective-permute-start = (bf16[512,4096]{1,0:T(8,128)(2,1)}, bf16[512,4096]{1,0:T(8,128)(2,1)}, u32[]{:S(2)}, u32[]{:S(2)}) collective-permute-start(bf16[512,4096]{1,0:T(8,128)(2,1)} %fusion.3), channel_id=1, source_target_pairs={{0,16},{16,32},{32,48},{48,0},{1,17},{17,33},{33,49},{49,1},{2,18}... | collective-permute-start | bytes 12582920 | tf_op jit(solution)/shard_map/ppermute | solution.py:10
Sparse Core Ops, SparseCore 0:
  27.3 152.9 all-reduce.1
